TPU v7x, 512 devices: a whole 4x4x16 slice. The times are simulated.
512 devices in a mesh: ctx: 16 (over y, x), head: 32 (over z, core).
Axes of the slice: x: 4, y: 4, z: 16, core: 2. Of those that a mesh axis runs over, the one named last changes fastest.
Arguments:
- doc_lengths: int32 [4], replicated, may hold values from 1 to 6144, 8192 in all
- lin_q: bfloat16 [8192, 8192], P('ctx', 'head'), may hold values from -6 to 6
- lin_k: bfloat16 [8192, 8192], P('ctx', 'head'), may hold values from -6 to 6
- lin_v: bfloat16 [8192, 8192], P('ctx', 'head'), may hold values from -40 to 40
- log_decay: float32 [64, 8192], P('head', 'ctx'), may hold values from -1 to 0
- lin_gain: float32 [8192], P('head'), may hold values from 0.5 to 1.5
- soft_q: bfloat16 [8192, 8192], P('ctx', 'head'), may hold values from -48 to 48
- soft_k: bfloat16 [8192, 1024], P('ctx', 'head'), may hold values from -6 to 6
- soft_v: bfloat16 [8192, 1024], P('ctx', 'head'), may hold values from -6 to 6
Outputs:
- lin_out: bfloat16 [8192, 8192], P('ctx', 'head')
- soft_out: bfloat16 [8192, 8192], P('ctx', 'head')
Inputs may be any that keep to these rules, and one draw needn't show every extreme that they name: `doc_lengths`: the 4 lengths sum to 8192 and the largest is exactly 6144.
All inputs are finite; a program needn't handle non-finite values.
Results may differ from a plain program's by a relative error of at most 0.015.
Values may be sent and summed in bfloat16 or wider, within the bound.
A program may use at most 64 MiB of HBM per device.

v0:
```python
import jax
import jax.numpy as jnp
from jax import lax
from jax.sharding import PartitionSpec as P

KVH = 8
DH = 128
BLK = 256


def prefix(value, axis, join, neutral):
    place = lax.axis_index(axis)
    gathered = jax.tree.map(
        lambda a, kind: lax.all_gather(a.astype(kind), axis), value, (jnp.bfloat16, jnp.bfloat16)
    )
    state = jax.tree.map(lambda a, e: jnp.zeros_like(a) + jnp.asarray(e, a.dtype), value, neutral)

    def one(turn, state):
        return join(
            state,
            jax.tree.map(
                lambda a, own: lax.dynamic_index_in_dim(a, turn, 0, False).astype(own.dtype),
                gathered,
                value,
            ),
        )

    return lax.fori_loop(0, place, one, state)


def swapped(value, axis, stride):
    return lax.ppermute(value, axis, [(i, i ^ 1 << stride) for i in range(lax.axis_size(axis))])


def doc_index(doc_lengths, positions):
    bounds = jnp.cumsum(doc_lengths)
    counted = jnp.sum((bounds[None, :] <= positions[:, None]).astype(jnp.int32), axis=1)
    return jnp.where(positions < 0, -1, counted)


def lightning_parts(queries, keys_block, values_block, decay_block, segs_block, seg_before):
    running = jnp.cumsum(decay_block, axis=1)
    block_len = segs_block.shape[0]
    rows_iota = lax.broadcasted_iota(jnp.int32, (block_len, block_len), 0)
    cols_iota = lax.broadcasted_iota(jnp.int32, (block_len, block_len), 1)
    allowed = (rows_iota >= cols_iota) & (segs_block[:, None] == segs_block[None, :])
    spread = jnp.where(allowed[None], running[:, :, None] - running[:, None, :], 0.0)
    decays = jnp.where(allowed[None], jnp.exp(spread), 0.0)
    scores = (
        jnp.einsum("ihd,jhd->hij", queries, keys_block, preferred_element_type=jnp.float32) * decays
    )
    scores = scores.astype(jnp.bfloat16)
    inside = jnp.einsum("hij,jhd->ihd", scores, values_block, preferred_element_type=jnp.float32)
    carried = (segs_block == seg_before).astype(jnp.float32)
    entering = jnp.exp(running) * carried[None, :]
    closing = running[:, -1:]
    tail_mask = (segs_block == segs_block[-1]).astype(jnp.float32)
    weights = jnp.exp(closing - running) * tail_mask[None, :]
    weighted = (keys_block * weights.T[:, :, None]).astype(jnp.bfloat16)
    update = jnp.einsum("jhd,jhe->hde", weighted, values_block, preferred_element_type=jnp.float32)
    kept_flag = (segs_block[-1] == seg_before).astype(jnp.float32)
    decay_factor = kept_flag * jnp.exp(closing[:, 0])
    return (inside, entering, update, decay_factor)


def local(doc_lengths, lin_q, lin_k, lin_v, log_decay, lin_gain, soft_q, soft_k, soft_v):
    tok_count = lin_q.shape[0]
    heads_here = lin_gain.shape[0] // DH
    ctx_place = lax.axis_index("ctx")
    positions = ctx_place * tok_count + jnp.arange(tok_count, dtype=jnp.int32)
    doc_ids = doc_index(doc_lengths, positions)
    seg_previous = doc_index(doc_lengths, positions[:1] - 1)[0]
    query_rows = lin_q.reshape(tok_count, heads_here, DH)
    key_rows = lin_k.reshape(tok_count, heads_here, DH)
    value_rows = lin_v.reshape(tok_count, heads_here, DH)
    blocks = tok_count // BLK
    pieces_list = []
    local_state = jnp.zeros((heads_here, DH, DH), jnp.float32)
    through = jnp.ones((heads_here,), jnp.float32)
    for number in range(blocks):
        first_row = number * BLK
        last_row = first_row + BLK
        seg_before = seg_previous if number == 0 else doc_ids[first_row - 1]
        parts_now = lightning_parts(
            query_rows[first_row:last_row],
            key_rows[first_row:last_row],
            value_rows[first_row:last_row],
            log_decay[:, first_row:last_row],
            doc_ids[first_row:last_row],
            seg_before,
        )
        pieces_list.append(parts_now)
        local_state = parts_now[3][:, None, None] * local_state + parts_now[2]
        through = through * parts_now[3]
    empty_state = jnp.zeros((heads_here, DH, DH), jnp.float32)

    def combine(earlier, later):
        return (earlier[0] * later[0], later[0][:, None, None] * earlier[1] + later[1])

    incoming = prefix(
        (through, local_state), "ctx", combine, (jnp.ones((heads_here,), jnp.float32), empty_state)
    )
    carry_state = incoming[1]
    outputs = []
    for number in range(blocks):
        first_row = number * BLK
        inside, entering, update, decay_factor = pieces_list[number]
        across = jnp.einsum(
            "ihd,hde->ihe",
            query_rows[first_row : first_row + BLK],
            carry_state.astype(jnp.bfloat16),
            preferred_element_type=jnp.float32,
        )
        outputs.append(inside + across * entering.T[:, :, None])
        carry_state = decay_factor[:, None, None] * carry_state + update
    raw_out = jnp.concatenate(outputs, axis=0)
    norm_scale = lax.rsqrt(jnp.mean(raw_out * raw_out, axis=2, keepdims=True) + 1e-06)
    lin_out = (
        (raw_out * norm_scale * lin_gain.reshape(1, heads_here, DH))
        .reshape(tok_count, heads_here * DH)
        .astype(jnp.bfloat16)
    )
    head_place = lax.axis_index("head")
    group_width = lax.axis_size("head") // KVH
    bit_count = group_width.bit_length() - 1
    own_keys, own_values = (soft_k, soft_v)
    for bit in range(bit_count):
        far_keys, far_values = swapped((own_keys, own_values), "head", bit)
        upper = head_place // (1 << bit) % 2 == 1
        own_keys = jnp.where(
            upper,
            jnp.concatenate([far_keys, own_keys], axis=1),
            jnp.concatenate([own_keys, far_keys], axis=1),
        )
        own_values = jnp.where(
            upper,
            jnp.concatenate([far_values, own_values], axis=1),
            jnp.concatenate([own_values, far_values], axis=1),
        )
    soft_rows = soft_q.reshape(tok_count, heads_here, DH)

    def attend(softmax_state, key_piece, value_piece, key_start):
        row_top, row_total, accum_rows = softmax_state
        key_pos = key_start + jnp.arange(key_piece.shape[0], dtype=jnp.int32)
        key_doc = doc_index(doc_lengths, key_pos)
        scores = jnp.einsum(
            "ihd,jd->hij", soft_rows, key_piece, preferred_element_type=jnp.float32
        ) * DH ** (-0.5)
        allowed = (key_pos[None, :] <= positions[:, None]) & (key_doc[None, :] == doc_ids[:, None])
        masked = jnp.where(allowed[None], scores, -1e30)
        new_top = jnp.maximum(row_top, jnp.max(masked, axis=2))
        exp_terms = jnp.where(allowed[None], jnp.exp(scores - new_top[:, :, None]), 0.0)
        rescale = jnp.exp(row_top - new_top)
        new_total = rescale * row_total + jnp.sum(exp_terms, axis=2)
        new_accum = rescale[:, :, None] * accum_rows + jnp.einsum(
            "hij,jd->hid",
            exp_terms.astype(jnp.bfloat16),
            value_piece,
            preferred_element_type=jnp.float32,
        )
        return (new_top, new_total, new_accum)

    def visit(softmax_state, key_piece, value_piece, key_start):
        return attend(softmax_state, key_piece, value_piece, key_start)

    start_state = (
        jnp.full((heads_here, tok_count), -1e30, jnp.float32),
        jnp.zeros((heads_here, tok_count), jnp.float32),
        jnp.zeros((heads_here, tok_count, DH), jnp.float32),
    )
    key_piece = lax.all_gather(own_keys, "ctx", axis=0, tiled=True)
    value_piece = lax.all_gather(own_values, "ctx", axis=0, tiled=True)
    row_count = key_piece.shape[0]

    def inner_visit(state_in, scan_items):
        offset, key_part, value_part = scan_items
        return (visit(state_in, key_part, value_part, offset), None)

    offsets = jnp.arange(row_count // 512, dtype=jnp.int32) * 512
    result, _ = lax.scan(
        inner_visit,
        start_state,
        (
            offsets,
            key_piece.reshape(row_count // 512, 512, DH),
            value_piece.reshape(row_count // 512, 512, DH),
        ),
    )
    final_top, final_total, final_accum = result
    soft_out = (
        (final_accum / final_total[:, :, None])
        .transpose(1, 0, 2)
        .reshape(tok_count, heads_here * DH)
        .astype(jnp.bfloat16)
    )
    return (lin_out, soft_out)


def solution(mesh):
    placed = (
        P(),
        P("ctx", "head"),
        P("ctx", "head"),
        P("ctx", "head"),
        P("head", "ctx"),
        P("head"),
        P("ctx", "head"),
        P("ctx", "head"),
        P("ctx", "head"),
    )
    return jax.shard_map(
        local,
        mesh=mesh,
        in_specs=placed,
        out_specs=(P("ctx", "head"), P("ctx", "head")),
        check_vma=False,
    )
```

profile of v0, /device:TPU:1, one launch (start us, length us, event | category | flops | bytes accessed | tf_op | source)
XLA Modules:
  0.0 323.4 jit_solution(9549522584730469660)
XLA Ops:
  7.8 0.8 reduce-window.19
  8.7 0.7 fusion.69
  12.6 1.3 compare_convert_fusion.1
  14.6 0.7 fusion.67
  17.8 1.0 fusion.65
  18.9 1.0 fusion.66
  20.6 0.8 fusion.33
  21.5 8.8 %collective-permute-start = (bf16[512,32]{0,1:T(8,128)(2,1)S(1)}, bf16[512,32]{0,1:T(8,128)(2,1)S(1)}, u32[]{:S(2)}, u32[]{:S(2)}) collective-permute-start(bf16[512,32]{0,1:T(8,128)(2,1)S(1)} %copy-done.2), channel_id=1, source_target_pairs={{0,1},{1,0},{2,3},{3,2},{4,5},{5,4},{6,7},{7,6},{8,9},{9,8},{10,11... | collective-permute-start | bytes 98312 | tf_op jit(solution)/shard_map/ppermute | solution.py:32
  30.3 0.8 collective-permute-done
  31.1 1.9 collective-permute-start.1
  33.1 3.1 collective-permute-done.1
  36.1 0.7 maximum_select_fusion
  36.9 3.4 %collective-permute-start.2 = (bf16[512,32]{0,1:T(8,128)(2,1)S(1)}, bf16[512,32]{0,1:T(8,128)(2,1)S(1)}, u32[]{:S(2)}, u32[]{:S(2)}) collective-permute-start(bf16[512,32]{0,1:T(8,128)(2,1)S(1)} %copy-done.3), channel_id=1, source_target_pairs={{0,1},{1,0},{2,3},{3,2},{4,5},{5,4},{6,7},{7,6},{8,9},{9,8},{10,11... | collective-permute-start | bytes 98312 | tf_op jit(solution)/shard_map/ppermute | solution.py:32
  40.3 0.8 collective-permute-done.2
  41.2 1.9 collective-permute-start.3
  43.1 3.1 collective-permute-done.3
  46.2 0.7 maximum_select_fusion.1
  46.9 1.3 dynamic-slice
  49.1 28.6 %all-reduce = bf16[32]{0:T(256)(128)(2,1)S(1)} all-reduce(bf16[32]{0:T(256)(128)(2,1)S(1)} %dynamic-update-slice), channel_id=2, replica_groups=mesh['ctx'=16,'head'=32] {'ctx'}, use_global_device_ids=true, to_apply=%add | all-reduce | flops 32 | bytes 128
  78.7 4.9 %all-gather.10.cloned.1.call-done = bf16[32,128,128]{2,1,0:T(8,128)(2,1)} async-done(((bf16[2,128,128]{2,1,0:T(8,128)(2,1)}), bf16[32,128,128]{2,1,0:T(8,128)(2,1)}) %all-gather.10.cloned.1.call-update) | async-done | bytes 1048592 | tf_op jit(solution)/shard_map/all_gather | solution.py:14
  86.3 0.8 fusion.35
  87.0 62.9 %all-gather.6.cloned.1.call-done = bf16[8192,128]{0,1:T(8,128)(2,1)} async-done(((bf16[512,128]{0,1:T(8,128)(2,1)}), bf16[8192,128]{0,1:T(8,128)(2,1)}) %all-gather.6.cloned.1.call-update) | async-done | bytes 2097168 | tf_op jit(solution)/shard_map/all_gather | solution.py:171
  150.0 4.1 %copy.122 = bf16[8192,128]{1,0:T(8,128)(2,1)} copy(bf16[8192,128]{0,1:T(8,128)(2,1)} %all-gather.6.cloned.1.call-done) | data formatting | bytes 4194304 | tf_op jit(solution)/shard_map/all_gather | solution.py:171
  154.1 61.4 %all-gather.8.cloned.1.call-done = bf16[8192,128]{0,1:T(8,128)(2,1)} async-done(((bf16[512,128]{0,1:T(8,128)(2,1)}), bf16[8192,128]{0,1:T(8,128)(2,1)}) %all-gather.8.cloned.1.call-update) | async-done | bytes 2097168 | tf_op jit(solution)/shard_map/all_gather | solution.py:172
  215.5 4.1 %copy.124 = bf16[8192,128]{1,0:T(8,128)(2,1)} copy(bf16[8192,128]{0,1:T(8,128)(2,1)} %all-gather.8.cloned.1.call-done) | data formatting | bytes 4194304 | tf_op jit(solution)/shard_map/all_gather | solution.py:172
  219.5 96.5 %while.30 = (s32[]{:T(128)}, f32[2,512]{1,0:T(2,128)S(1)}, f32[2,512]{1,0:T(2,128)S(1)}, f32[2,512,128]{2,1,0:T(8,128)S(1)}, s32[16]{0:T(128)S(1)}, /*index=5*/s...) while((s32[]{:T(128)}, f32[2,512]{1,0:T(2,128)S(1)}, ...), condition=%wide.region_15.16_spmd.clone, body=%wide.region_11.15_spmd.clone.sunk | while | flops 275395584 | bytes 9000113 | solution.py:180
  220.9 0.6 compare_select_fusion.3
  221.8 1.5 fusion.92
  223.8 1.7 convolution_add_fusion.3
  226.9 0.6 compare_select_fusion.3
  227.8 1.5 fusion.92
  229.8 1.7 convolution_add_fusion.3
  232.9 0.6 compare_select_fusion.3
  233.9 1.5 fusion.92
  235.9 1.7 convolution_add_fusion.3
  238.9 0.6 compare_select_fusion.3
  239.9 1.5 fusion.92
  241.9 1.7 convolution_add_fusion.3
  245.9 1.5 fusion.92
  247.9 1.7 convolution_add_fusion.3
  252.0 1.5 fusion.92
  253.9 1.7 convolution_add_fusion.3
  258.0 1.5 fusion.92
  260.0 1.7 convolution_add_fusion.3
  264.0 1.5 fusion.92
  266.0 1.7 convolution_add_fusion.3
  270.0 1.5 fusion.92
  272.0 1.7 convolution_add_fusion.3
  276.1 1.5 fusion.92
  278.1 1.7 convolution_add_fusion.3
  282.1 1.5 fusion.92
  284.1 1.7 convolution_add_fusion.3
  288.1 1.5 fusion.92
  290.1 1.7 convolution_add_fusion.3
  294.2 1.5 fusion.92
  296.2 1.7 convolution_add_fusion.3
  299.2 0.6 compare_select_fusion.3
  300.2 1.5 fusion.92
  302.2 1.7 convolution_add_fusion.3
  306.2 1.5 fusion.92
  308.2 1.7 convolution_add_fusion.3
  312.2 1.5 fusion.92
  314.2 1.7 convolution_add_fusion.3
  316.0 0.9 copy_bitcast_fusion
  (215 shorter events, 49.4 us)
Async XLA Ops:
  7.2 14.3 %copy-start.2 = (bf16[512,32]{0,1:T(8,128)(2,1)S(1)}, bf16[512,32]{0,1:T(8,128)(2,1)}, u32[]{:S(2)}) copy-start(bf16[512,32]{0,1:T(8,128)(2,1)} %param.20) | copy-start | bytes 98308
  7.2 29.7 %copy-start.3 = (bf16[512,32]{0,1:T(8,128)(2,1)S(1)}, bf16[512,32]{0,1:T(8,128)(2,1)}, u32[]{:S(2)}) copy-start(bf16[512,32]{0,1:T(8,128)(2,1)} %param.21) | copy-start | bytes 98308
  7.2 76.5 %all-gather.10.cloned.1.call-start = ((), (), s32[]{:S(2)}) async-start(), calls=%async_computation.2 | async-start | bytes 1114112 | tf_op jit(solution)/shard_map/all_gather | solution.py:14
  17.8 59.9 %copy-start = (bf16[512,256]{1,0:T(8,128)(2,1)S(1)}, bf16[512,256]{1,0:T(8,128)(2,1)}, u32[]{:S(2)}) copy-start(bf16[512,256]{1,0:T(8,128)(2,1)} %param.19) | copy-start | bytes 786436
  19.9 58.1 %copy-start.5 = (s32[4]{0:T(128)S(1)}, s32[4]{0:T(128)}, u32[]{:S(2)}) copy-start(s32[4]{0:T(128)} %param.13) | copy-start | bytes 52
  19.9 58.4 %copy-start.1 = (bf16[512,256]{1,0:T(8,128)(2,1)S(1)}, bf16[512,256]{1,0:T(8,128)(2,1)}, u32[]{:S(2)}) copy-start(bf16[512,256]{1,0:T(8,128)(2,1)} %param.14) | copy-start | bytes 786436
  21.4 128.6 %all-gather.6.cloned.1.call-start = ((), (), s32[]{:S(2)}) async-start(), calls=%async_computation | async-start | bytes 2228224 | tf_op jit(solution)/shard_map/all_gather | solution.py:171
  21.5 9.6 %collective-permute-start = (bf16[512,32]{0,1:T(8,128)(2,1)S(1)}, bf16[512,32]{0,1:T(8,128)(2,1)S(1)}, u32[]{:S(2)}, u32[]{:S(2)}) collective-permute-start(bf16[512,32]{0,1:T(8,128)(2,1)S(1)} %copy-done.2), channel_id=1, source_target_pairs={{0,1},{1,0},{2,3},{3,2},{4,5},{5,4},{6,7},{7,6},{8,9},{9,8},{10,11... | collective-permute-start | bytes 98312 | tf_op jit(solution)/shard_map/ppermute | solution.py:32
  31.1 5.0 %collective-permute-start.1 = (bf16[512,64]{0,1:T(8,128)(2,1)S(1)}, bf16[512,64]{0,1:T(8,128)(2,1)S(1)}, u32[]{:S(2)}, u32[]{:S(2)}) collective-permute-start(bf16[512,64]{0,1:T(8,128)(2,1)S(1)} %maximum_select_fusion.2), channel_id=1, source_target_pairs={{0,2},{1,3},{2,0},{3,1},{4,6},{5,7},{6,4},{7,5},{8,10},{9,11},{10,... | collective-permute-start | bytes 196616 | tf_op jit(solution)/shard_map/ppermute | solution.py:32
  36.8 178.6 %all-gather.8.cloned.1.call-start = ((), (), s32[]{:S(2)}) async-start(), calls=%async_computation.1 | async-start | bytes 2228224 | tf_op jit(solution)/shard_map/all_gather | solution.py:172
  36.9 4.3 %collective-permute-start.2 = (bf16[512,32]{0,1:T(8,128)(2,1)S(1)}, bf16[512,32]{0,1:T(8,128)(2,1)S(1)}, u32[]{:S(2)}, u32[]{:S(2)}) collective-permute-start(bf16[512,32]{0,1:T(8,128)(2,1)S(1)} %copy-done.3), channel_id=1, source_target_pairs={{0,1},{1,0},{2,3},{3,2},{4,5},{5,4},{6,7},{7,6},{8,9},{9,8},{10,11... | collective-permute-start | bytes 98312 | tf_op jit(solution)/shard_map/ppermute | solution.py:32
  41.2 5.0 %collective-permute-start.3 = (bf16[512,64]{0,1:T(8,128)(2,1)S(1)}, bf16[512,64]{0,1:T(8,128)(2,1)S(1)}, u32[]{:S(2)}, u32[]{:S(2)}) collective-permute-start(bf16[512,64]{0,1:T(8,128)(2,1)S(1)} %maximum_select_fusion.3), channel_id=1, source_target_pairs={{0,2},{1,3},{2,0},{3,1},{4,6},{5,7},{6,4},{7,5},{8,10},{9,11},{10,... | collective-permute-start | bytes 196616 | tf_op jit(solution)/shard_map/ppermute | solution.py:32
  84.7 1.6 copy-start.4
Sparse Core Ops, SparseCore 0:
  21.5 62.0 all-gather.9
  87.2 62.7 all-gather.5
  153.0 62.4 all-gather.7
where the time goes:
time: 326 us; the launch traced here: 323 us
  waiting for transfers between devices  137 us (42%)
  matrix products  53.5 us (16%)
  other arithmetic  43.1 us (13%)
  blocking collectives  28.6 us (9%)
  local copies, waits for them, and re-layouts  25.8 us (8%)
  between operations  18.1 us (6%)
  starting transfers between devices  16.2 us (5%)
    all_gather x1, waiting for transfers between devices, local(): key_piece = lax.all_gather(own_keys, 'ctx', axis=0, tiled=True)  62.9 us
    all_gather x1, waiting for transfers between devices, local(): value_piece = lax.all_gather(own_values, 'ctx', axis=0, tiled=True)  61.4 us
    unnamed x1, blocking collectives  28.6 us
    dot_general x16, matrix products, attend(): jnp.einsum('hij,jd->hid', exp_terms.astype(jnp.bfloat16), value_piece, pr...  27.7 us
    dot_general x16, matrix products, attend(): jnp.einsum('ihd,jd->hij', soft_rows, key_piece, preferred_element_type=jn...  23.3 us
    ppermute x4, starting transfers between devices, swapped(): lax.ppermute(value, axis, [(i, i ^ 1 << stride) for i in range(lax.axis_s...  16 us
    select_n x17, other arithmetic, doc_index(): return jnp.where(positions < 0, -1, counted)  10.4 us
    add x17, other arithmetic, local(): positions = ctx_place * tok_count + jnp.arange(tok_count, dtype=jnp.int32)  10.4 us
  transfers between devices with their start and end apart: 7, of which 7 were waited for; matrix products, arithmetic and copies ran while one was open for 3% of the time, Pallas kernels for 0%

commit v1 on v0

--- a/solution.py
+++ b/solution.py
@@ -169,7 +169,12 @@
         jnp.zeros((heads_here, tok_count, DH), jnp.float32),
     )
     key_piece = lax.all_gather(own_keys, "ctx", axis=0, tiled=True)
-    value_piece = lax.all_gather(own_values, "ctx", axis=0, tiled=True)
+    ring = [own_values]
+    for hop in range(15):
+        ring.append(lax.ppermute(ring[-1], "ctx", [(dev, (dev + 1) % 16) for dev in range(16)]))
+    value_piece = jnp.roll(
+        jnp.concatenate(ring[::-1], axis=0), (lax.axis_index("ctx") + 1) * ring[0].shape[0], axis=0
+    )
     row_count = key_piece.shape[0]
 
     def inner_visit(state_in, scan_items):

time: 326 us -> 388 us (1.19)
  starting transfers between devices: 16.2 us -> 55.1 us
  local copies, waits for them, and re-layouts: 25.8 us -> 34.9 us
  blocking collectives: 28.6 us -> 34.2 us
  other arithmetic: 43.1 us -> 48.5 us
  matrix products: 53.5 us -> 58.6 us
    ppermute x0 -> x15, waiting for transfers between devices: none -> 77.7 us  [local(): lax.ppermute(ring[-1], 'ctx', [(dev, (dev + 1) % 16) for dev in range(16)])]
    all_gather x1 -> x0, waiting for transfers between devices: 61.4 us -> none  [local(): value_piece = lax.all_gather(own_values, 'ctx', axis=0, tiled=True)]
    ppermute x0 -> x15, starting transfers between devices: none -> 28.7 us  [local(): lax.ppermute(ring[-1], 'ctx', [(dev, (dev + 1) % 16) for dev in range(16)])]
    ppermute x4, starting transfers between devices: 16 us -> 26.4 us  [swapped(): lax.ppermute(value, axis, [(i, i ^ 1 << stride) for i in range(lax.axis_s...]
    unnamed x26 -> x59, local copies, waits for them, and re-layouts: 2.62 us -> 10.9 us
    all_gather x1, waiting for transfers between devices: 62.9 us -> 55.6 us  [local(): key_piece = lax.all_gather(own_keys, 'ctx', axis=0, tiled=True)]
    ppermute x4, waiting for transfers between devices: 7.79 us -> 0.79 us  [swapped(): lax.ppermute(value, axis, [(i, i ^ 1 << stride) for i in range(lax.axis_s...]
    unnamed x1, blocking collectives: 28.6 us -> 34.2 us
  transfers between devices with their start and end apart: 7 -> 21, of which waited for: 7 -> 14; matrix products, arithmetic and copies ran while one was open for 3% -> 11% of each run, Pallas kernels for 0% -> 0%
where the time goes in v1:
time: 388 us; the launch traced here: 385 us
  waiting for transfers between devices  134 us (35%)
  matrix products  58.6 us (15%)
  starting transfers between devices  55.1 us (14%)
  other arithmetic  48.5 us (12%)
  local copies, waits for them, and re-layouts  34.9 us (9%)
  blocking collectives  34.2 us (9%)
  between operations  18.7 us (5%)
    ppermute x15, waiting for transfers between devices, local(): lax.ppermute(ring[-1], 'ctx', [(dev, (dev + 1) % 16) for dev in range(16)])  77.7 us
    all_gather x1, waiting for transfers between devices, local(): key_piece = lax.all_gather(own_keys, 'ctx', axis=0, tiled=True)  55.6 us
    unnamed x1, blocking collectives  34.2 us
    ppermute x15, starting transfers between devices, local(): lax.ppermute(ring[-1], 'ctx', [(dev, (dev + 1) % 16) for dev in range(16)])  28.7 us
    dot_general x16, matrix products, attend(): jnp.einsum('hij,jd->hid', exp_terms.astype(jnp.bfloat16), value_piece, pr...  27.7 us
    ppermute x4, starting transfers between devices, swapped(): lax.ppermute(value, axis, [(i, i ^ 1 << stride) for i in range(lax.axis_s...  26.4 us
    dot_general x16, matrix products, attend(): jnp.einsum('ihd,jd->hij', soft_rows, key_piece, preferred_element_type=jn...  23.3 us
    unnamed x59, local copies, waits for them, and re-layouts  10.9 us
  transfers between devices with their start and end apart: 21, of which 14 were waited for; matrix products, arithmetic and copies ran while one was open for 11% of the time, Pallas kernels for 0%

profile of v1, /device:TPU:1, one launch (start us, length us, event | category | flops | bytes accessed | tf_op | source)
XLA Modules:
  0.0 385.2 jit_solution(15965211139263131461)
XLA Ops:
  7.2 8.8 %collective-permute-start.2 = (bf16[512,32]{0,1:T(8,128)(2,1)}, bf16[512,32]{0,1:T(8,128)(2,1)S(1)}, u32[]{:S(2)}, u32[]{:S(2)}) collective-permute-start(bf16[512,32]{0,1:T(8,128)(2,1)} %param.21), channel_id=1, source_target_pairs={{0,1},{1,0},{2,3},{3,2},{4,5},{5,4},{6,7},{7,6},{8,9},{9,8},{10,11... | collective-permute-start | bytes 98312 | tf_op jit(solution)/shard_map/ppermute | solution.py:32
  26.9 1.9 collective-permute-start.3
  32.6 1.9 collective-permute-start.4
  35.1 6.9 %collective-permute-done.4 = bf16[512,128]{0,1:T(8,128)(2,1)S(1)} collective-permute-done((bf16[512,128]{0,1:T(8,128)(2,1)S(1)}, bf16[512,128]{0,1:T(8,128)(2,1)S(1)}, u32[]{:S(2)}, u32[]{:S(2)}) %collective-permute-start.4) | collective-permute-done | bytes 131104 | tf_op jit(solution)/shard_map/ppermute | solution.py:174
  42.0 1.9 collective-permute-start.5
  44.1 6.9 %collective-permute-done.5 = bf16[512,128]{0,1:T(8,128)(2,1)S(1)} collective-permute-done((bf16[512,128]{0,1:T(8,128)(2,1)S(1)}, bf16[512,128]{0,1:T(8,128)(2,1)S(1)}, u32[]{:S(2)}, u32[]{:S(2)}) %collective-permute-start.5) | collective-permute-done | bytes 131104 | tf_op jit(solution)/shard_map/ppermute | solution.py:174
  51.0 1.9 collective-permute-start.6
  53.5 6.5 %collective-permute-done.6 = bf16[512,128]{0,1:T(8,128)(2,1)S(1)} collective-permute-done((bf16[512,128]{0,1:T(8,128)(2,1)S(1)}, bf16[512,128]{0,1:T(8,128)(2,1)S(1)}, u32[]{:S(2)}, u32[]{:S(2)}) %collective-permute-start.6) | collective-permute-done | bytes 131104 | tf_op jit(solution)/shard_map/ppermute | solution.py:174
  60.0 1.9 collective-permute-start.7
  62.9 6.2 %collective-permute-done.7 = bf16[512,128]{0,1:T(8,128)(2,1)S(1)} collective-permute-done((bf16[512,128]{0,1:T(8,128)(2,1)S(1)}, bf16[512,128]{0,1:T(8,128)(2,1)S(1)}, u32[]{:S(2)}, u32[]{:S(2)}) %collective-permute-start.7) | collective-permute-done | bytes 131104 | tf_op jit(solution)/shard_map/ppermute | solution.py:174
  69.1 1.9 collective-permute-start.8
  71.0 7.1 %collective-permute-done.8 = bf16[512,128]{0,1:T(8,128)(2,1)S(1)} collective-permute-done((bf16[512,128]{0,1:T(8,128)(2,1)S(1)}, bf16[512,128]{0,1:T(8,128)(2,1)S(1)}, u32[]{:S(2)}, u32[]{:S(2)}) %collective-permute-start.8) | collective-permute-done | bytes 131104 | tf_op jit(solution)/shard_map/ppermute | solution.py:174
  78.1 1.9 collective-permute-start.9
  80.0 7.2 %collective-permute-done.9 = bf16[512,128]{0,1:T(8,128)(2,1)S(1)} collective-permute-done((bf16[512,128]{0,1:T(8,128)(2,1)S(1)}, bf16[512,128]{0,1:T(8,128)(2,1)S(1)}, u32[]{:S(2)}, u32[]{:S(2)}) %collective-permute-start.9) | collective-permute-done | bytes 131104 | tf_op jit(solution)/shard_map/ppermute | solution.py:174
  87.2 1.9 collective-permute-start.10
  89.1 7.1 %collective-permute-done.10 = bf16[512,128]{0,1:T(8,128)(2,1)S(1)} collective-permute-done((bf16[512,128]{0,1:T(8,128)(2,1)S(1)}, bf16[512,128]{0,1:T(8,128)(2,1)S(1)}, u32[]{:S(2)}, u32[]{:S(2)}) %collective-permute-start.10) | collective-permute-done | bytes 131104 | tf_op jit(solution)/shard_map/ppermute | solution.py:174
  96.2 1.9 collective-permute-start.11
  98.1 7.4 %collective-permute-done.11 = bf16[512,128]{0,1:T(8,128)(2,1)S(1)} collective-permute-done((bf16[512,128]{0,1:T(8,128)(2,1)S(1)}, bf16[512,128]{0,1:T(8,128)(2,1)S(1)}, u32[]{:S(2)}, u32[]{:S(2)}) %collective-permute-start.11) | collective-permute-done | bytes 131104 | tf_op jit(solution)/shard_map/ppermute | solution.py:174
  105.6 1.9 collective-permute-start.12
  107.5 13.3 %collective-permute-start = (bf16[512,32]{0,1:T(8,128)(2,1)}, bf16[512,32]{0,1:T(8,128)(2,1)S(1)}, u32[]{:S(2)}, u32[]{:S(2)}) collective-permute-start(bf16[512,32]{0,1:T(8,128)(2,1)} %param.20), channel_id=1, source_target_pairs={{0,1},{1,0},{2,3},{3,2},{4,5},{5,4},{6,7},{7,6},{8,9},{9,8},{10,11... | collective-permute-start | bytes 98312 | tf_op jit(solution)/shard_map/ppermute | solution.py:32
  120.8 1.9 collective-permute-start.13
  122.8 1.7 fusion.64
  124.5 5.7 %collective-permute-done.13 = bf16[512,128]{0,1:T(8,128)(2,1)S(1)} collective-permute-done((bf16[512,128]{0,1:T(8,128)(2,1)S(1)}, bf16[512,128]{0,1:T(8,128)(2,1)S(1)}, u32[]{:S(2)}, u32[]{:S(2)}) %collective-permute-start.13) | collective-permute-done | bytes 131104 | tf_op jit(solution)/shard_map/ppermute | solution.py:174
  130.2 1.9 collective-permute-start.14
  132.1 7.1 %collective-permute-done.14 = bf16[512,128]{0,1:T(8,128)(2,1)S(1)} collective-permute-done((bf16[512,128]{0,1:T(8,128)(2,1)S(1)}, bf16[512,128]{0,1:T(8,128)(2,1)S(1)}, u32[]{:S(2)}, u32[]{:S(2)}) %collective-permute-start.14) | collective-permute-done | bytes 131104 | tf_op jit(solution)/shard_map/ppermute | solution.py:174
  139.2 1.9 collective-permute-start.15
  141.9 6.3 %collective-permute-done.15 = bf16[512,128]{0,1:T(8,128)(2,1)S(1)} collective-permute-done((bf16[512,128]{0,1:T(8,128)(2,1)S(1)}, bf16[512,128]{0,1:T(8,128)(2,1)S(1)}, u32[]{:S(2)}, u32[]{:S(2)}) %collective-permute-start.15) | collective-permute-done | bytes 131104 | tf_op jit(solution)/shard_map/ppermute | solution.py:174
  148.2 1.9 collective-permute-start.16
  152.9 2.3 collective-permute-start.1
  155.3 3.2 collective-permute-done.16
  158.4 1.9 collective-permute-start.17
  160.9 34.2 %all-reduce = bf16[32]{0:T(256)(128)(2,1)} all-reduce(bf16[32]{0:T(256)(128)(2,1)S(1)} %dynamic-update-slice), channel_id=2, replica_groups=mesh['ctx'=16,'head'=32] {'ctx'}, use_global_device_ids=true, to_apply=%add | all-reduce | flops 32 | bytes 128
  199.1 1.7 copy.144
  200.8 1.6 maximum_select_fusion
  202.5 1.9 collective-permute-start.18
  204.5 1.6 fusion.32
  206.1 1.5 fusion.29
  207.6 1.9 fusion.31
  209.5 1.5 fusion.30
  212.1 1.5 fusion.35
  218.9 2.4 copy.124
  221.3 55.6 %all-gather.5.cloned.1.call-done = bf16[8192,128]{0,1:T(8,128)(2,1)} async-done(((bf16[512,128]{0,1:T(8,128)(2,1)}), bf16[8192,128]{0,1:T(8,128)(2,1)}) %all-gather.5.cloned.1.call-update) | async-done | bytes 2097168 | tf_op jit(solution)/shard_map/all_gather | solution.py:171
  276.9 4.1 %copy.122 = bf16[8192,128]{1,0:T(8,128)(2,1)} copy(bf16[8192,128]{0,1:T(8,128)(2,1)} %all-gather.5.cloned.1.call-done) | data formatting | bytes 4194304 | tf_op jit(solution)/shard_map/all_gather | solution.py:171
  281.0 96.5 %while.30 = (s32[]{:T(128)}, f32[2,512]{1,0:T(2,128)S(1)}, f32[2,512]{1,0:T(2,128)S(1)}, f32[2,512,128]{2,1,0:T(8,128)S(1)}, s32[16]{0:T(128)S(1)}, /*index=5*/s...) while((s32[]{:T(128)}, f32[2,512]{1,0:T(2,128)S(1)}, ...), condition=%wide.region_15.16_spmd.clone, body=%wide.region_11.15_spmd.clone.sunk | while | flops 275395584 | bytes 9000113 | solution.py:185
  283.3 1.5 fusion.92
  285.3 1.7 convolution_add_fusion.3
  289.3 1.5 fusion.92
  291.3 1.7 convolution_add_fusion.3
  297.3 1.7 convolution_add_fusion.3
  303.4 1.7 convolution_add_fusion.3
  307.4 1.5 fusion.92
  309.4 1.7 convolution_add_fusion.3
  315.4 1.7 convolution_add_fusion.3
  321.5 1.7 convolution_add_fusion.3
  325.5 1.5 fusion.92
  327.5 1.7 convolution_add_fusion.3
  333.5 1.7 convolution_add_fusion.3
  339.5 1.7 convolution_add_fusion.3
  345.6 1.7 convolution_add_fusion.3
  351.6 1.7 convolution_add_fusion.3
  357.6 1.7 convolution_add_fusion.3
  363.7 1.7 convolution_add_fusion.3
  369.7 1.7 convolution_add_fusion.3
  375.7 1.7 convolution_add_fusion.3
  (277 shorter events, 89.8 us)
Async XLA Ops:
  7.2 145.1 %copy-start.3 = (bf16[512,32]{0,1:T(8,128)(2,1)S(1)}, bf16[512,32]{0,1:T(8,128)(2,1)}, u32[]{:S(2)}) copy-start(bf16[512,32]{0,1:T(8,128)(2,1)} %param.20) | copy-start | bytes 98308
  7.2 197.2 %all-gather.7.cloned.1.call-start = ((), (), s32[]{:S(2)}) async-start(), calls=%async_computation.1 | async-start | bytes 1114112 | tf_op jit(solution)/shard_map/all_gather | solution.py:14
  7.2 18.9 %collective-permute-start.2 = (bf16[512,32]{0,1:T(8,128)(2,1)}, bf16[512,32]{0,1:T(8,128)(2,1)S(1)}, u32[]{:S(2)}, u32[]{:S(2)}) collective-permute-start(bf16[512,32]{0,1:T(8,128)(2,1)} %param.21), channel_id=1, source_target_pairs={{0,1},{1,0},{2,3},{3,2},{4,5},{5,4},{6,7},{7,6},{8,9},{9,8},{10,11... | collective-permute-start | bytes 98312 | tf_op jit(solution)/shard_map/ppermute | solution.py:32
  26.9 5.6 %collective-permute-start.3 = (bf16[512,64]{0,1:T(8,128)(2,1)S(1)}, bf16[512,64]{0,1:T(8,128)(2,1)S(1)}, u32[]{:S(2)}, u32[]{:S(2)}) collective-permute-start(bf16[512,64]{0,1:T(8,128)(2,1)S(1)} %maximum_select_fusion.3), channel_id=1, source_target_pairs={{0,2},{1,3},{2,0},{3,1},{4,6},{5,7},{6,4},{7,5},{8,10},{9,11},{10,... | collective-permute-start | bytes 196616 | tf_op jit(solution)/shard_map/ppermute | solution.py:32
  31.0 0.8 copy-start.4
  31.1 3.4 copy-start.5
  32.6 9.4 %collective-permute-start.4 = (bf16[512,128]{0,1:T(8,128)(2,1)S(1)}, bf16[512,128]{0,1:T(8,128)(2,1)S(1)}, u32[]{:S(2)}, u32[]{:S(2)}) collective-permute-start(bf16[512,128]{0,1:T(8,128)(2,1)S(1)} %maximum_select_fusion.1), channel_id=1, source_target_pairs={{0,32},{32,64},{64,96},{96,128},{128,160},{160,192},{192,224},{224... | collective-permute-start | bytes 393224 | tf_op jit(solution)/shard_map/ppermute | solution.py:174
  42.0 9.0 %collective-permute-start.5 = (bf16[512,128]{0,1:T(8,128)(2,1)S(1)}, bf16[512,128]{0,1:T(8,128)(2,1)S(1)}, u32[]{:S(2)}, u32[]{:S(2)}) collective-permute-start(bf16[512,128]{0,1:T(8,128)(2,1)S(1)} %collective-permute-done.4), channel_id=1, source_target_pairs={{0,32},{32,64},{64,96},{96,128},{128,160},{160,192},{192,224},{224... | collective-permute-start | bytes 393224 | tf_op jit(solution)/shard_map/ppermute | solution.py:174
  51.0 9.0 %collective-permute-start.6 = (bf16[512,128]{0,1:T(8,128)(2,1)S(1)}, bf16[512,128]{0,1:T(8,128)(2,1)S(1)}, u32[]{:S(2)}, u32[]{:S(2)}) collective-permute-start(bf16[512,128]{0,1:T(8,128)(2,1)S(1)} %collective-permute-done.5), channel_id=1, source_target_pairs={{0,32},{32,64},{64,96},{96,128},{128,160},{160,192},{192,224},{224... | collective-permute-start | bytes 393224 | tf_op jit(solution)/shard_map/ppermute | solution.py:174
  60.0 9.0 %collective-permute-start.7 = (bf16[512,128]{0,1:T(8,128)(2,1)S(1)}, bf16[512,128]{0,1:T(8,128)(2,1)S(1)}, u32[]{:S(2)}, u32[]{:S(2)}) collective-permute-start(bf16[512,128]{0,1:T(8,128)(2,1)S(1)} %collective-permute-done.6), channel_id=1, source_target_pairs={{0,32},{32,64},{64,96},{96,128},{128,160},{160,192},{192,224},{224... | collective-permute-start | bytes 393224 | tf_op jit(solution)/shard_map/ppermute | solution.py:174
  62.8 214.1 %all-gather.5.cloned.1.call-start = ((), (), s32[]{:S(2)}) async-start(), calls=%async_computation | async-start | bytes 2228224 | tf_op jit(solution)/shard_map/all_gather | solution.py:171
  69.1 9.0 %collective-permute-start.8 = (bf16[512,128]{0,1:T(8,128)(2,1)S(1)}, bf16[512,128]{0,1:T(8,128)(2,1)S(1)}, u32[]{:S(2)}, u32[]{:S(2)}) collective-permute-start(bf16[512,128]{0,1:T(8,128)(2,1)S(1)} %collective-permute-done.7), channel_id=1, source_target_pairs={{0,32},{32,64},{64,96},{96,128},{128,160},{160,192},{192,224},{224... | collective-permute-start | bytes 393224 | tf_op jit(solution)/shard_map/ppermute | solution.py:174
  78.1 9.1 %collective-permute-start.9 = (bf16[512,128]{0,1:T(8,128)(2,1)S(1)}, bf16[512,128]{0,1:T(8,128)(2,1)S(1)}, u32[]{:S(2)}, u32[]{:S(2)}) collective-permute-start(bf16[512,128]{0,1:T(8,128)(2,1)S(1)} %collective-permute-done.8), channel_id=1, source_target_pairs={{0,32},{32,64},{64,96},{96,128},{128,160},{160,192},{192,224},{224... | collective-permute-start | bytes 393224 | tf_op jit(solution)/shard_map/ppermute | solution.py:174
  87.2 9.1 %collective-permute-start.10 = (bf16[512,128]{0,1:T(8,128)(2,1)S(1)}, bf16[512,128]{0,1:T(8,128)(2,1)S(1)}, u32[]{:S(2)}, u32[]{:S(2)}) collective-permute-start(bf16[512,128]{0,1:T(8,128)(2,1)S(1)} %collective-permute-done.9), channel_id=1, source_target_pairs={{0,32},{32,64},{64,96},{96,128},{128,160},{160,192},{192,224},{224... | collective-permute-start | bytes 393224 | tf_op jit(solution)/shard_map/ppermute | solution.py:174
  96.2 9.4 %collective-permute-start.11 = (bf16[512,128]{0,1:T(8,128)(2,1)S(1)}, bf16[512,128]{0,1:T(8,128)(2,1)S(1)}, u32[]{:S(2)}, u32[]{:S(2)}) collective-permute-start(bf16[512,128]{0,1:T(8,128)(2,1)S(1)} %collective-permute-done.10), channel_id=1, source_target_pairs={{0,32},{32,64},{64,96},{96,128},{128,160},{160,192},{192,224},{224... | collective-permute-start | bytes 393224 | tf_op jit(solution)/shard_map/ppermute | solution.py:174
  105.6 15.3 %collective-permute-start.12 = (bf16[512,128]{0,1:T(8,128)(2,1)S(1)}, bf16[512,128]{0,1:T(8,128)(2,1)S(1)}, u32[]{:S(2)}, u32[]{:S(2)}) collective-permute-start(bf16[512,128]{0,1:T(8,128)(2,1)S(1)} %collective-permute-done.11), channel_id=1, source_target_pairs={{0,32},{32,64},{64,96},{96,128},{128,160},{160,192},{192,224},{224... | collective-permute-start | bytes 393224 | tf_op jit(solution)/shard_map/ppermute | solution.py:174
  107.5 44.8 %collective-permute-start = (bf16[512,32]{0,1:T(8,128)(2,1)}, bf16[512,32]{0,1:T(8,128)(2,1)S(1)}, u32[]{:S(2)}, u32[]{:S(2)}) collective-permute-start(bf16[512,32]{0,1:T(8,128)(2,1)} %param.20), channel_id=1, source_target_pairs={{0,1},{1,0},{2,3},{3,2},{4,5},{5,4},{6,7},{7,6},{8,9},{9,8},{10,11... | collective-permute-start | bytes 98312 | tf_op jit(solution)/shard_map/ppermute | solution.py:32
  120.8 9.3 %collective-permute-start.13 = (bf16[512,128]{0,1:T(8,128)(2,1)S(1)}, bf16[512,128]{0,1:T(8,128)(2,1)S(1)}, u32[]{:S(2)}, u32[]{:S(2)}) collective-permute-start(bf16[512,128]{0,1:T(8,128)(2,1)S(1)} %collective-permute-done.12), channel_id=1, source_target_pairs={{0,32},{32,64},{64,96},{96,128},{128,160},{160,192},{192,224},{224... | collective-permute-start | bytes 393224 | tf_op jit(solution)/shard_map/ppermute | solution.py:174
  130.2 9.0 %collective-permute-start.14 = (bf16[512,128]{0,1:T(8,128)(2,1)S(1)}, bf16[512,128]{0,1:T(8,128)(2,1)S(1)}, u32[]{:S(2)}, u32[]{:S(2)}) collective-permute-start(bf16[512,128]{0,1:T(8,128)(2,1)S(1)} %collective-permute-done.13), channel_id=1, source_target_pairs={{0,32},{32,64},{64,96},{96,128},{128,160},{160,192},{192,224},{224... | collective-permute-start | bytes 393224 | tf_op jit(solution)/shard_map/ppermute | solution.py:174
  139.2 9.0 %collective-permute-start.15 = (bf16[512,128]{0,1:T(8,128)(2,1)S(1)}, bf16[512,128]{0,1:T(8,128)(2,1)S(1)}, u32[]{:S(2)}, u32[]{:S(2)}) collective-permute-start(bf16[512,128]{0,1:T(8,128)(2,1)S(1)} %collective-permute-done.14), channel_id=1, source_target_pairs={{0,32},{32,64},{64,96},{96,128},{128,160},{160,192},{192,224},{224... | collective-permute-start | bytes 393224 | tf_op jit(solution)/shard_map/ppermute | solution.py:174
  148.2 10.2 %collective-permute-start.16 = (bf16[512,128]{0,1:T(8,128)(2,1)S(1)}, bf16[512,128]{0,1:T(8,128)(2,1)S(1)}, u32[]{:S(2)}, u32[]{:S(2)}) collective-permute-start(bf16[512,128]{0,1:T(8,128)(2,1)S(1)} %collective-permute-done.15), channel_id=1, source_target_pairs={{0,32},{32,64},{64,96},{96,128},{128,160},{160,192},{192,224},{224... | collective-permute-start | bytes 393224 | tf_op jit(solution)/shard_map/ppermute | solution.py:174
  152.9 47.9 %collective-permute-start.1 = (bf16[512,64]{0,1:T(8,128)(2,1)}, bf16[512,64]{0,1:T(8,128)(2,1)}, u32[]{:S(2)}, u32[]{:S(2)}) collective-permute-start(bf16[512,64]{0,1:T(8,128)(2,1)} %maximum_select_fusion.2), channel_id=1, source_target_pairs={{0,2},{1,3},{2,0},{3,1},{4,6},{5,7},{6,4},{7,5},{8,10},{9,11},{10,... | collective-permute-start | bytes 196616 | tf_op jit(solution)/shard_map/ppermute | solution.py:32
  158.4 46.0 %copy-start = (bf16[512,128]{0,1:T(8,128)(2,1)}, bf16[512,128]{0,1:T(8,128)(2,1)S(1)}, u32[]{:S(2)}) copy-start(bf16[512,128]{0,1:T(8,128)(2,1)S(1)} %collective-permute-done.16) | copy-start | bytes 393220
  158.4 44.0 %collective-permute-start.17 = (bf16[512,128]{0,1:T(8,128)(2,1)S(1)}, bf16[512,128]{0,1:T(8,128)(2,1)}, u32[]{:S(2)}, u32[]{:S(2)}) collective-permute-start(bf16[512,128]{0,1:T(8,128)(2,1)S(1)} %collective-permute-done.16), channel_id=1, source_target_pairs={{0,32},{32,64},{64,96},{96,128},{128,160},{160,192},{192,224},{224... | collective-permute-start | bytes 393224 | tf_op jit(solution)/shard_map/ppermute | solution.py:174
  199.1 7.0 %copy-start.2 = (bf16[256,256]{0,1:T(8,128)(2,1)}, bf16[256,256]{0,1:T(8,128)(2,1)S(1)}, u32[]{:S(2)}) copy-start(bf16[256,256]{0,1:T(8,128)(2,1)S(1)} %copy.138) | copy-start | bytes 393220
  202.5 11.1 %collective-permute-start.18 = (bf16[512,128]{0,1:T(8,128)(2,1)}, bf16[512,128]{0,1:T(8,128)(2,1)}, u32[]{:S(2)}, u32[]{:S(2)}) collective-permute-start(bf16[512,128]{0,1:T(8,128)(2,1)} %collective-permute-done.17), channel_id=1, source_target_pairs={{0,32},{32,64},{64,96},{96,128},{128,160},{160,192},{192,224},{224... | collective-permute-start | bytes 393224 | tf_op jit(solution)/shard_map/ppermute | solution.py:174
  211.5 6.9 %copy-start.1 = (bf16[512,128]{0,1:T(8,128)(2,1)S(1)}, bf16[512,128]{0,1:T(8,128)(2,1)}, u32[]{:S(2)}) copy-start(bf16[512,128]{0,1:T(8,128)(2,1)} %copy-done) | copy-start | bytes 393220
  218.9 62.2 %copy-start.6 = (s32[16]{0:T(128)S(1)}, s32[16]{0:T(128)}, u32[]{:S(2)}) copy-start(s32[16]{0:T(128)} %iota_multiply_fusion) | copy-start | bytes 196
Sparse Core Ops, SparseCore 0:
  62.9 61.5 all-gather.6
  202.6 74.3 all-gather.4
